TPU v7x, 256 devices: a whole 4x4x8 slice. The times are simulated.
256 devices in a mesh: dp: 64 (over x, y, z_hi), tensor: 4 (over z_lo, core).
Axes of the slice: x: 4, y: 4, z: 8 (z_hi: 4, z_lo: 2; z = z_hi * 2 + z_lo), core: 2. Of those that a mesh axis runs over, the one named last changes fastest.
Arguments:
- tokens: bfloat16 [32768, 6144], P('dp', 'tensor'), may hold values from -6 to 6
- block_mask: int32 [128, 4, 4], P('dp'), may hold values from 0 to 1
- norm_gain: float32 [6144], replicated, may hold values from 0.25 to 1.75
- w_query: bfloat16 [6144, 3072], P('dp', 'tensor'), may hold values from -0.078125 to 0.078125
- w_key: bfloat16 [6144, 3072], P('dp', 'tensor'), may hold values from -0.078125 to 0.078125
- w_value: bfloat16 [6144, 3072], P('dp', 'tensor'), may hold values from -0.078125 to 0.078125
- query_gain: float32 [128], replicated, may hold values from 0.1 to 1.9
- key_gain: float32 [128], replicated, may hold values from 0.1 to 1.9
Outputs:
- attended: bfloat16 [32768, 3072], P('dp', 'tensor')
All inputs are finite; a program needn't handle non-finite values.
Results may differ from a plain program's by a relative error of at most 0.0085.
Values may be sent and summed in bfloat16 or wider, within the bound.
A program may use at most 192 MiB of HBM per device.

v0:
```python
import jax
import jax.numpy as jnp
from jax import lax
from jax.sharding import PartitionSpec as P

DH = 128
TPD = 256
BLOCK = 64


EPS = 1e-06


def sent_together(arrays, axis, dim, along):
    widths = [a.shape[along] for a in arrays]
    both = jnp.concatenate(arrays, axis=along)
    whole = lax.all_gather(both, axis, axis=dim, tiled=True)
    return tuple(jnp.split(whole, [sum(widths[:k]) for k in range(1, len(widths))], axis=along))


def layer_norm(rows, gain):
    values = rows.astype(jnp.float32)
    mean = jnp.mean(values, axis=-1, keepdims=True)
    mean_sq = jnp.mean(values * values, axis=-1, keepdims=True)
    return (values - mean) * lax.rsqrt(mean_sq - mean * mean + EPS) * gain


def head_norm(values, gain):
    mean_sq = jnp.mean(values * values, axis=-1, keepdims=True)
    return values * lax.rsqrt(mean_sq + EPS) * gain


def add_rows(normed, piece):
    return jnp.dot(normed, piece, preferred_element_type=jnp.float32)


def per_device(tokens, block_mask, norm_gain, w_query, w_key, w_value, query_gain, key_gain):
    whole = lax.all_gather(tokens, "tensor", axis=1, tiled=True)
    normed = layer_norm(whole, norm_gain).astype(jnp.bfloat16)
    pieces = sent_together((w_query, w_key, w_value), "dp", 0, 1)
    query = add_rows(normed, pieces[0])
    key = add_rows(normed, pieces[1])
    value = add_rows(normed, pieces[2])
    draws_here = tokens.shape[0] // TPD
    heads_here = w_query.shape[1] // DH
    query_n = head_norm(query.reshape(draws_here, TPD, heads_here, DH), query_gain).astype(
        jnp.bfloat16
    )
    key_n = head_norm(key.reshape(draws_here, TPD, heads_here, DH), key_gain).astype(jnp.bfloat16)
    value = value.astype(jnp.bfloat16).reshape(draws_here, TPD, heads_here, DH)
    blocks = block_mask.shape[-1]
    allowed = (block_mask > 0) | (jnp.arange(blocks)[:, None] == jnp.arange(blocks)[None, :])[None]
    allowed = jnp.repeat(jnp.repeat(allowed, BLOCK, axis=1), BLOCK, axis=2)
    scores = jnp.einsum(
        "bqhe,bkhe->bhqk", query_n, key_n, preferred_element_type=jnp.float32
    ) / jnp.sqrt(jnp.float32(DH))
    scores = jnp.where(allowed[:, None], scores, jnp.float32(-1e30))
    top = jnp.max(scores, axis=-1, keepdims=True)
    weights = jnp.exp(scores - top)
    probs = (weights / jnp.sum(weights, axis=-1, keepdims=True)).astype(jnp.bfloat16)
    out = jnp.einsum("bhqk,bkhe->bqhe", probs, value, preferred_element_type=jnp.float32)
    return out.astype(jnp.bfloat16).reshape(tokens.shape[0], heads_here * DH)


def solution(mesh):
    return jax.shard_map(
        per_device,
        mesh=mesh,
        in_specs=(
            P("dp", "tensor"),
            P("dp", None, None),
            P(),
            P("dp", "tensor"),
            P("dp", "tensor"),
            P("dp", "tensor"),
            P(),
            P(),
        ),
        out_specs=P("dp", "tensor"),
        check_vma=False,
    )
```

profile of v0, /device:TPU:1, one launch (start us, length us, event | category | flops | bytes accessed | tf_op | source)
XLA Modules:
  0.0 384.6 jit_solution(3754338296619104776)
XLA Ops:
  6.5 0.0 copy-start.3
  6.5 0.0 all-gather.3.cloned.1.call-start
  6.5 0.7 all-gather.3.cloned.1.call-update
  7.3 0.0 all-gather.5.cloned.1.call-start
  7.3 1.8 pad_maximum_fusion
  9.2 0.0 all-gather.5.cloned.1.call-update
  9.2 0.7 compare_or_fusion
  9.9 0.1 copy.15
  10.0 0.1 broadcast_in_dim.14
  10.1 0.1 reshape.68
  10.2 69.8 %all-gather.3.cloned.1.call-done = bf16[512,6144]{1,0:T(8,128)(2,1)} async-done(((bf16[512,1536]{1,0:T(8,128)(2,1)}), bf16[512,6144]{1,0:T(8,128)(2,1)}) %all-gather.3.cloned.1.call-update) | async-done | bytes 6291472 | tf_op jit(solution)/shard_map/all_gather | solution.py:38
  80.0 4.8 %convert_reduce_fusion = (f32[512]{0:T(512)S(1)}, f32[512]{0:T(512)S(1)}) fusion(bf16[512,6144]{1,0:T(8,128)(2,1)} %all-gather.3.cloned.1.call-done), kind=kLoop, calls=%fused_computation.3 | loop fusion | flops 12581888 | bytes 6295552 | tf_op jit(solution)/shard_map/reduce_sum | solution.py:23
  84.8 246.9 %all-gather.5.cloned.1.call-done = bf16[6144,2304]{1,0:T(8,128)(2,1)} async-done(((bf16[96,2304]{1,0:T(8,128)(2,1)}), bf16[6144,2304]{1,0:T(8,128)(2,1)}) %all-gather.5.cloned.1.call-update) | async-done | bytes 28311568 | tf_op jit(solution)/shard_map/all_gather | solution.py:17
  331.7 0.0 copy-done.3
  331.7 10.9 %fusion.17 = bf16[512,768]{1,0:T(8,128)(2,1)S(1)} fusion(bf16[6144,2304]{1,0:T(8,128)(2,1)} %all-gather.5.cloned.1.call-done, bf16[512,6144]{1,0:T(8,128)(2,1)} %all-gather.3.cloned.1.call-done, f32[6144]{0:T(1024)S(1)} %copy-done.3, f32[512]{0:T(512)S(1)} %get-tuple-element.8, f32[512]{0:T(512)S(1)} %get-tuple-element.7), kind=kOutput, calls=%fused_computation.27 | convolution fusion | flops 4847960064 | bytes 16543744 | tf_op jit(solution)/shard_map/dot_general | solution.py:34
  342.5 1.9 reshape.72
  344.4 10.9 %fusion.7 = f32[512,768]{0,1:T(8,128)S(1)} fusion(bf16[6144,2304]{1,0:T(8,128)(2,1)} %all-gather.5.cloned.1.call-done, bf16[512,6144]{1,0:T(8,128)(2,1)} %all-gather.3.cloned.1.call-done, f32[6144]{0:T(1024)S(1)} %copy-done.3, f32[512]{0:T(512)S(1)} %get-tuple-element.8, f32[512]{0:T(512)S(1)} %get-tuple-element.7), kind=kOutput, calls=%fused_computation.10 | convolution fusion | flops 4847566848 | bytes 17330176 | tf_op jit(solution)/shard_map/dot_general | solution.py:34
  355.4 1.0 reshape.69
  356.4 12.0 %fusion.5 = f32[512,768]{0,1:T(8,128)} fusion(bf16[6144,2304]{1,0:T(8,128)(2,1)} %all-gather.5.cloned.1.call-done, bf16[512,6144]{1,0:T(8,128)(2,1)} %all-gather.3.cloned.1.call-done, f32[6144]{0:T(1024)S(1)} %copy-done.3, f32[512]{0:T(512)S(1)} %get-tuple-element.8, f32[512]{0:T(512)S(1)} %get-tuple-element.7), kind=kOutput, calls=%fused_computation.8 | convolution fusion | flops 4847566848 | bytes 17330176 | tf_op jit(solution)/shard_map/dot_general | solution.py:34
  368.4 0.0 copy-start.1
  368.4 0.0 copy-start.2
  368.4 2.3 reshape.70
  370.7 0.6 multiply_reduce_fusion
  371.3 0.6 multiply_reduce_fusion.1
  372.0 0.0 copy-done.1
  372.0 0.0 copy-done.2
  372.0 1.6 multiply_convert_fusion
  373.6 0.0 copy-start
  373.7 0.6 fusion.22
  374.3 1.1 fusion.30
  375.4 0.0 copy-done
  375.4 0.5 fusion.20
  375.9 0.8 copy.29
  376.7 1.0 copy.39
  (5 shorter events, 0.1 us)
Async XLA Ops:
  6.5 325.1 %copy-start.3 = (f32[6144]{0:T(1024)S(1)}, f32[6144]{0:T(1024)}, u32[]{:S(2)}) copy-start(f32[6144]{0:T(1024)} %param.10) | copy-start | bytes 73732
  6.5 73.4 %all-gather.3.cloned.1.call-start = ((), (), s32[]{:S(2)}) async-start(), calls=%async_computation | async-start | bytes 7864320 | tf_op jit(solution)/shard_map/all_gather | solution.py:38
  7.3 324.4 %all-gather.5.cloned.1.call-start = ((), (), s32[]{:S(2)}) async-start(), calls=%async_computation.1 | async-start | bytes 28753920 | tf_op jit(solution)/shard_map/all_gather | solution.py:17
  368.4 3.6 copy-start.1
  368.4 3.6 copy-start.2
  373.6 1.8 copy-start
Sparse Core Ops, SparseCore 0:
  9.1 70.7 all-gather.2
  83.2 248.4 all-gather.4
where the time goes:
time: 385 us
  waiting for transfers between devices  317 us (82%)
  matrix products  34.9 us (9%)
  between operations  13.5 us (4%)
  other arithmetic  11.4 us (3%)
  local copies, waits for them, and re-layouts  7.26 us (2%)
    all_gather x1, waiting for transfers between devices, sent_together(): whole = lax.all_gather(both, axis, axis=dim, tiled=True)  247 us
    all_gather x1, waiting for transfers between devices, per_device(): whole = lax.all_gather(tokens, 'tensor', axis=1, tiled=True)  69.8 us
    dot_general x3, matrix products, add_rows(): return jnp.dot(normed, piece, preferred_element_type=jnp.float32)  33.8 us
  transfers between devices with their start and end apart: 2, of which 2 were waited for; matrix products, arithmetic and copies ran while one was open for 2% of the time, Pallas kernels for 0%

commit v1 on v0

v1 whole, which is shorter than its diff:
```python
import jax
import jax.numpy as jnp
from jax import lax
from jax.experimental import pallas as pl
from jax.experimental.pallas import tpu as pltpu
from jax.sharding import PartitionSpec as P

DH = 128
TPD = 256
BLOCK = 64
EPS = 1e-06
MESH = pl.DeviceIdType.MESH

ROWS = 96
FEAT = 1536
D = 6144
NC = 384
N = 3 * NC

AXP, AXM, AZ = 0, 2, 4
AD, AL, AOP, AOM = 6, 7, 8, 9
AIIP, AIIM, AIII = 10, 12, 14
MK = 16
SW = 19
ZP, ZM, ZFP, ZFM = 21, 23, 25, 26
YP, YM = 27, 35
YFP, YFM = 43, 47
DO = 51
DYM, DYP, DYO = 59, 61, 63
OUT = 65
COUNT = 69


def kernel(tok, mk, gn, wq, wk, wv, qg, kg, out, a_buf, b_buf, ws, acc, s1, s2, cs, mbuf, obuf, ssem, rsem):
    dp = lax.axis_index("dp")
    t = lax.axis_index("tensor")
    x, y, zh = dp // 16, (dp // 4) % 4, dp % 4
    zlo, c = t // 2, t % 2
    xp, xm, xo = (x + 1) % 4, (x + 3) % 4, (x + 2) % 4
    yp, ym, yo = (y + 1) % 4, (y + 3) % 4, (y + 2) % 4
    zp, zm, zo = (zh + 1) % 4, (zh + 3) % 4, (zh + 2) % 4

    def dev(x_=None, y_=None, zh_=None, zlo_=None, c_=None):
        x_ = x if x_ is None else x_
        y_ = y if y_ is None else y_
        zh_ = zh if zh_ is None else zh_
        zlo_ = zlo if zlo_ is None else zlo_
        c_ = c if c_ is None else c_
        return (x_ * 16 + y_ * 4 + zh_, zlo_ * 2 + c_)

    def remote(src, dst, sid, rid, device):
        return pltpu.make_async_remote_copy(
            src_ref=src, dst_ref=dst, send_sem=ssem.at[sid], recv_sem=rsem.at[rid], device_id=device, device_id_type=MESH
        )

    def a_at(xb, q):
        return a_buf.at[pl.ds(pl.multiple_of(xb * TPD, TPD), TPD), pl.ds(pl.multiple_of(q * FEAT, FEAT), FEAT)]

    def b_at(xw, yw, zw, n=1):
        return b_buf.at[pl.ds(pl.multiple_of(((xw * 4 + yw) * 4 + zw) * ROWS, ROWS), n * ROWS), :]

    def got(ref, rid):
        remote(ref, ref, 0, rid, dev(c_=1 - c)).wait_recv()

    def sent(ref, sid):
        remote(ref, ref, sid, 0, dev(c_=1 - c)).wait_send()

    for e in range(2):
        for p, w in enumerate((wq, wk, wv)):
            for j in range(3):
                cols = slice(e * NC + j * 128, e * NC + (j + 1) * 128)
                ws[e, :, p * NC + j * 128 : p * NC + (j + 1) * 128] = (w[:, cols].astype(jnp.float32) * gn[...]).astype(jnp.bfloat16)
    mbuf[x] = mk[...]

    barrier = pltpu.get_barrier_semaphore()
    for dx in range(4):
        for dc in range(2):
            if dx or dc:
                pl.semaphore_signal(barrier, inc=1, device_id=dev(x_=(x + dx) % 4, c_=(c + dc) % 2), device_id_type=MESH)
    for core in range(2):
        pl.semaphore_signal(barrier, inc=1, device_id=dev(zlo_=1 - zlo, c_=core), device_id_type=MESH)
    for other in (dev(y_=yp), dev(y_=ym), dev(zh_=zp), dev(zh_=zm)):
        pl.semaphore_signal(barrier, inc=1, device_id=other, device_id_type=MESH)
    pl.semaphore_wait(barrier, 13)

    def swap(e):
        here = b_at(x, y, zh)
        away = jnp.logical_or(c + 2 * e != x, x // 2 != c)
        return away, remote(ws.at[e], here, SW + e, SW + x % 2, dev(x_=c + 2 * e, c_=x // 2)), pltpu.make_async_copy(
            ws.at[e], here, rsem.at[SW + x % 2]
        )

    for e in range(2):
        away, far, near = swap(e)

        @pl.when(away)
        def _():
            far.start()

        @pl.when(jnp.logical_not(away))
        def _():
            near.start()

    def first(r, dst_dev, base):
        return remote(tok.at[pl.ds(r * TPD, TPD), :], a_at(x, t), base + r, base + c, dst_dev)

    for r in range(2):
        first(r, dev(x_=xp, c_=r), AXP).start()
        first(r, dev(x_=xm, c_=r), AXM).start()
    across = remote(tok.at[pl.ds(pl.multiple_of((1 - c) * TPD, TPD), TPD), :], a_at(x, t), AD, AD, dev(c_=1 - c))
    across.start()
    own = pltpu.make_async_copy(tok.at[pl.ds(pl.multiple_of(c * TPD, TPD), TPD), :], a_at(x, t), rsem.at[AL])
    own.start()
    for k in range(3):
        remote(mk, mbuf.at[x], MK + k, MK + k, dev(x_=(x + k + 1) % 4)).start()

    xw = [2 * c, 2 * c + 1]

    def y_out(k, z):
        for h in range(2):
            piece = b_at(xw[h], y, z)
            remote(piece, piece, YP + 2 * k + h, YP + 2 * k + h, dev(y_=yp)).start()
            remote(piece, piece, YM + 2 * k + h, YM + 2 * k + h, dev(y_=ym)).start()
            remote(piece, piece, DO + 2 * k + h, DO + 2 * k + h, dev(c_=1 - c)).start()

    for h in range(2):
        piece = b_at(xw[h], y, zh)
        got(piece, SW + h)
        remote(piece, piece, ZP + h, ZP + h, dev(zh_=zp)).start()
        remote(piece, piece, ZM + h, ZM + h, dev(zh_=zm)).start()
    y_out(0, zh)

    acc[...] = jnp.zeros_like(acc)
    s1[...] = jnp.zeros_like(s1)
    s2[...] = jnp.zeros_like(s2)

    for h in range(2):
        got(b_at(xw[h], y, zm), ZP + h)
    piece = b_at(xw[0], y, zm)
    remote(piece, piece, ZFP, ZFP, dev(zh_=zp)).start()
    for h in range(2):
        got(b_at(xw[h], y, zp), ZM + h)
    piece = b_at(xw[1], y, zp)
    remote(piece, piece, ZFM, ZFM, dev(zh_=zm)).start()
    for r in range(2):
        first(r, dev(zlo_=1 - zlo, c_=r), AZ).start()
    y_out(1, zm)
    y_out(2, zp)
    got(b_at(xw[0], y, zo), ZFP)
    got(b_at(xw[1], y, zo), ZFM)
    y_out(3, zo)

    zs = [zh, zp, zm, zo]

    def y_step(k):
        z = [zh, zm, zp, zo][k]
        for h in range(2):
            got(b_at(xw[h], ym, z), YP + 2 * k + h)
        piece = b_at(xw[0], ym, z)
        remote(piece, piece, YFP + k, YFP + k, dev(y_=yp)).start()
        for h in range(2):
            got(b_at(xw[h], yp, z), YM + 2 * k + h)
        piece = b_at(xw[1], yp, z)
        remote(piece, piece, YFM + k, YFM + k, dev(y_=ym)).start()

    y_step(0)
    y_step(1)
    for q in range(2):
        got(a_at(xm, 2 * zlo + q), AXP + q)
        got(a_at(xp, 2 * zlo + q), AXM + q)
    piece = a_at(xm, 2 * zlo)
    remote(piece, piece, AOP, AOP, dev(x_=xp)).start()
    piece = a_at(xp, 2 * zlo + 1)
    remote(piece, piece, AOM, AOM, dev(x_=xm)).start()
    y_step(2)
    for q in range(2):
        piece = a_at(x, 2 * (1 - zlo) + q)
        got(piece, AZ + q)
        remote(piece, piece, AIIP + q, AIIP + q, dev(x_=xp)).start()
        remote(piece, piece, AIIM + q, AIIM + q, dev(x_=xm)).start()
    y_step(3)
    for base, yy in ((DYM, ym), (DYP, yp)):
        for h in range(2):
            chunk = b_at(xw[h], yy, 0, 4)
            remote(chunk, chunk, base + h, base + h, dev(c_=1 - c)).start()
    for q, num in enumerate((AOP, AOM)):
        piece = a_at(xo, 2 * zlo + q)
        got(piece, num)
        remote(piece, piece, AIII + q, AIII + q, dev(zlo_=1 - zlo)).start()
    for h, num in enumerate((YFP, YFM)):
        for k in range(4):
            got(b_at(xw[h], yo, [zh, zm, zp, zo][k]), num + k)
        chunk = b_at(xw[h], yo, 0, 4)
        remote(chunk, chunk, DYO + h, DYO + h, dev(c_=1 - c)).start()
    xv = [2 * (1 - c), 2 * (1 - c) + 1]
    for h in range(2):
        for k in range(4):
            got(b_at(xv[h], y, [zh, zm, zp, zo][k]), DO + 2 * k + h)
    for base, yy in ((DYM, ym), (DYP, yp), (DYO, yo)):
        for h in range(2):
            got(b_at(xv[h], yy, 0, 4), base + h)
    got(a_at(x, 2 * zlo + 1 - c), AD)
    own.wait()
    for k in range(3):
        got(mbuf.at[(x + 3 - k) % 4], MK + k)

    def add_cols(i, total):
        rows = b_buf[pl.ds(pl.multiple_of(i * 32, 32), 32), :].astype(jnp.float32)
        return total + (rows[:8] + rows[8:16]) + (rows[16:24] + rows[24:])

    total = lax.fori_loop(0, D // 32, add_cols, jnp.zeros((8, N), jnp.float32))
    cs[...] = jnp.broadcast_to(jnp.sum(total, axis=0, keepdims=True), (8, N))

    def unit(xb, q):
        row = pl.multiple_of(xb * TPD, TPD)
        col = pl.multiple_of(q * FEAT, FEAT)
        acc[pl.ds(row, TPD), :] += jnp.dot(
            a_buf[pl.ds(row, TPD), pl.ds(col, FEAT)], b_buf[pl.ds(col, FEAT), :], preferred_element_type=jnp.float32
        )

        def stat(i, _):
            rr = pl.multiple_of(row + i * 64, 64)
            t1 = s1[pl.ds(rr, 64), :]
            t2 = s2[pl.ds(rr, 64), :]
            for j in range(FEAT // 128):
                v = a_buf[pl.ds(rr, 64), pl.ds(pl.multiple_of(col + j * 128, 128), 128)].astype(jnp.float32)
                t1 = t1 + v
                t2 = t2 + v * v
            s1[pl.ds(rr, 64), :] = t1
            s2[pl.ds(rr, 64), :] = t2
            return 0

        lax.fori_loop(0, TPD // 64, stat, 0)

    def order(i):
        return (x + jnp.where(i == 1, 3, jnp.where(i == 2, 1, jnp.where(i == 3, 2, 0)))) % 4

    def near(i, _):
        unit(order(i // 2), 2 * zlo + i % 2)
        return 0

    lax.fori_loop(0, 8, near, 0)

    def out_copy(xb, i):
        src = obuf.at[i]
        dst = out.at[pl.ds(pl.multiple_of(c * TPD, TPD), TPD), pl.ds(pl.multiple_of((x // 2) * NC, NC), NC)]
        rid = OUT + 2 * (x // 2) + c
        away = jnp.logical_or(xb != x, x % 2 != c)
        return away, remote(src, dst, OUT + i, rid, dev(x_=xb, c_=x % 2)), pltpu.make_async_copy(src, dst, rsem.at[rid])

    def finish(i, _):
        xb = order(i)
        for k, (num, blk) in enumerate(((AIIP, xm), (AIIM, xp), (AIII, xo))):

            @pl.when(i == k + 1)
            def _():
                for q in range(2):
                    got(a_at(blk, 2 * (1 - zlo) + q), num + q)

        def rest(q, _):
            unit(xb, 2 * (1 - zlo) + q)
            return 0

        lax.fori_loop(0, 2, rest, 0)
        row = pl.multiple_of(xb * TPD, TPD)
        mean = jnp.sum(s1[pl.ds(row, TPD), :], axis=-1, keepdims=True) * (1.0 / D)
        mean_sq = jnp.sum(s2[pl.ds(row, TPD), :], axis=-1, keepdims=True) * (1.0 / D)
        rstd = lax.rsqrt(mean_sq - mean * mean + EPS)

        def part(p, j):
            cols = slice(p * NC + j * DH, p * NC + (j + 1) * DH)
            return (acc[pl.ds(row, TPD), cols] - mean * cs[0:1, cols]) * rstd

        def head_norm(values, gain):
            ms = jnp.mean(values * values, axis=-1, keepdims=True)
            return (values * lax.rsqrt(ms + EPS) * gain).astype(jnp.bfloat16)

        allowed = mbuf[xb]
        seen = jnp.concatenate(
            [jnp.broadcast_to(jnp.where(c == 0, allowed[b : b + 1], allowed[8 + b : 9 + b]), (BLOCK, TPD)) for b in range(4)], axis=0
        )
        for j in range(3):
            qn = head_norm(part(0, j), qg[...])
            kn = head_norm(part(1, j), kg[...])
            v = part(2, j).astype(jnp.bfloat16)
            s = lax.dot_general(qn, kn, (((1,), (1,)), ((), ())), preferred_element_type=jnp.float32) * (1.0 / DH**0.5)
            s = jnp.where(seen > 0, s, jnp.float32(-1e30))
            w = jnp.exp(s - jnp.max(s, axis=-1, keepdims=True))
            probs = (w / jnp.sum(w, axis=-1, keepdims=True)).astype(jnp.bfloat16)
            obuf[i, :, j * DH : (j + 1) * DH] = jnp.dot(probs, v, preferred_element_type=jnp.float32).astype(jnp.bfloat16)
        away, far, near_ = out_copy(xb, i)

        @pl.when(away)
        def _():
            far.start()

        @pl.when(jnp.logical_not(away))
        def _():
            near_.start()

        return 0

    lax.fori_loop(0, 4, finish, 0)

    for e in range(2):
        for r in range(2):
            got(out.at[pl.ds(r * TPD, TPD), pl.ds(e * NC, NC)], OUT + 2 * e + r)
    a_piece = a_at(x, t)
    b_piece = b_at(x, y, zh)
    for num in (AXP, AXP + 1, AXM, AXM + 1, AZ, AZ + 1, AD, AOP, AOM, AIIP, AIIP + 1, AIIM, AIIM + 1, AIII, AIII + 1):
        sent(a_piece, num)
    for k in range(3):
        sent(mk, MK + k)
    for e in range(2):
        away, far, _ = swap(e)

        @pl.when(away)
        def _():
            far.wait_send()

    for num in range(ZP, DYM):
        sent(b_piece, num)
    for num in range(DYM, OUT):
        sent(b_at(x, y, 0, 4), num)
    for i in range(4):
        away, far, _ = out_copy(order(i), i)

        @pl.when(away)
        def _():
            far.wait_send()


def per_device(tokens, block_mask, norm_gain, w_query, w_key, w_value, query_gain, key_gain):
    blocks = block_mask.shape[-1]
    allowed = (block_mask > 0) | (jnp.arange(blocks)[:, None] == jnp.arange(blocks)[None, :])[None]
    allowed = jnp.repeat(allowed.astype(jnp.float32), BLOCK, axis=2)
    allowed = jnp.pad(allowed, ((0, 0), (0, 8 - blocks), (0, 0))).reshape(16, TPD)
    gain = lax.dynamic_slice(norm_gain, (lax.axis_index("dp") * ROWS,), (ROWS,))
    gain = jnp.broadcast_to(gain[:, None], (ROWS, 128))
    vmem = pl.BlockSpec(memory_space=pltpu.VMEM)
    return pl.pallas_call(
        kernel,
        out_shape=jax.ShapeDtypeStruct((512, 768), jnp.bfloat16),
        in_specs=[pl.BlockSpec(memory_space=pl.ANY)] + [vmem] * 7,
        out_specs=pl.BlockSpec(memory_space=pl.ANY),
        scratch_shapes=[
            pltpu.VMEM((4 * TPD, D), jnp.bfloat16),
            pltpu.VMEM((D, N), jnp.bfloat16),
            pltpu.VMEM((2, ROWS, N), jnp.bfloat16),
            pltpu.VMEM((4 * TPD, N), jnp.float32),
            pltpu.VMEM((4 * TPD, 128), jnp.float32),
            pltpu.VMEM((4 * TPD, 128), jnp.float32),
            pltpu.VMEM((8, N), jnp.float32),
            pltpu.VMEM((4, 16, TPD), jnp.float32),
            pltpu.VMEM((4, TPD, NC), jnp.bfloat16),
            pltpu.SemaphoreType.DMA((COUNT,)),
            pltpu.SemaphoreType.DMA((COUNT,)),
        ],
        compiler_params=pltpu.CompilerParams(collective_id=0, has_side_effects=True, vmem_limit_bytes=60 << 20),
    )(tokens, allowed, gain, w_query, w_key, w_value, query_gain.reshape(1, DH), key_gain.reshape(1, DH))


def solution(mesh):
    return jax.shard_map(
        per_device,
        mesh=mesh,
        in_specs=(
            P("dp", "tensor"),
            P("dp", None, None),
            P(),
            P("dp", "tensor"),
            P("dp", "tensor"),
            P("dp", "tensor"),
            P(),
            P(),
        ),
        out_specs=P("dp", "tensor"),
        check_vma=False,
    )
```

time: 385 us -> 135 us (0.35)
  waiting for transfers between devices: 317 us -> 0 us
  Pallas kernels: 0 us -> 128 us
  matrix products: 34.9 us -> 0 us
  between operations: 13.5 us -> 0.01 us
  other arithmetic: 11.4 us -> 0.7 us
    all_gather x2 -> x0, waiting for transfers between devices: 317 us -> none  [the longest x1 247 us: sent_together(): whole = lax.all_gather(both, axis, axis=dim, tiled=True)]
    pallas_call x0 -> x1, Pallas kernels: none -> 128 us  [per_device(): pl.pallas_call(kernel, out_shape=jax.ShapeDtypeStruct((512, 768), jnp.bfl...]
    dot_general x5 -> x0, matrix products: 34.9 us -> none  [the longest x3 33.8 us: add_rows(): return jnp.dot(normed, piece, preferred_element_type=jnp.float32)]
    reduce_sum x3 -> x0, other arithmetic: 6.06 us -> none  [the longest x1 4.83 us: layer_norm(): mean = jnp.mean(values, axis=-1, keepdims=True)]
    reshape x5 -> x2, local copies, waits for them, and re-layouts: 6 us -> 0.7 us  [the longest x1 0.61 us: per_device(): jnp.pad(allowed, ((0, 0), (0, 8 - blocks), (0, 0))).reshape(16, TPD)]
  transfers between devices with their start and end apart: 2 -> 0, of which waited for: 2 -> 0; matrix products, arithmetic and copies ran while one was open for 2% -> 0% of each run, Pallas kernels for 0% -> 0%
where the time goes in v1:
time: 135 us; the launch traced here: 133 us
  Pallas kernels  128 us (95%)
  local copies, waits for them, and re-layouts  4.3 us (3%)
    pallas_call x1, Pallas kernels, per_device(): pl.pallas_call(kernel, out_shape=jax.ShapeDtypeStruct((512, 768), jnp.bfl...  128 us

profile of v1, /device:TPU:1, one launch (start us, length us, event | category | flops | bytes accessed | tf_op | source)
XLA Modules:
  0.0 132.8 jit_solution(13084930938943687641)
XLA Ops:
  0.0 0.8 dynamic_slice.3
  0.8 0.7 or_convert_fusion
  1.5 0.1 broadcast_in_dim.4
  1.5 0.1 reshape.25
  1.6 0.6 pad_bitcast_fusion.mk
  2.2 0.7 broadcast_in_dim.5.gn
  2.9 127.8 %shard_map.82 = bf16[512,768]{1,0:T(8,128)(2,1)} custom-call(bf16[512,1536]{1,0:T(8,128)(2,1)} %tok.1, f32[16,256]{1,0:T(8,128)} %pad_bitcast_fusion.mk, f32[96,128]{1,0:T(8,128)} %broadcast_in_dim.5.gn, bf16[96,768]{1,0:T(8,128)(2,1)} %wq.1, bf16[96,768]{1,0:T(8,128)(2,1)} %wk.1, bf16[96,768]{1,0:T(8,128)(2,1)} %wv.1, f32[1,128]{1,0:T(1,128)} %bitcast.4, ...), custom_call_target="tpu_custom_call" | custom-call | tf_op jit(solution)/shard_map/pallas_call | solution.py:341
  130.8 2.1 %copy.10 = bf16[512,768]{1,0:T(8,128)(2,1)} copy(bf16[512,768]{1,0:T(8,128)(2,1)} %shard_map.82) | data formatting | bytes 1572864
  (1 shorter events, 0.0 us)

commit v2 on v1

v2 whole, which is shorter than its diff:
```python
import jax
import jax.numpy as jnp
from jax import lax
from jax.experimental import pallas as pl
from jax.experimental.pallas import tpu as pltpu
from jax.sharding import PartitionSpec as P

DH = 128
TPD = 256
BLOCK = 64
EPS = 1e-06
MESH = pl.DeviceIdType.MESH

ROWS = 96
FEAT = 1536
D = 6144
NC = 384
N = 3 * NC

AXP, AXM, AZ, AZL = 0, 2, 4, 6
AD, AL, AOP, AOM = 8, 9, 10, 11
AIIP, AIIM, AIII = 12, 14, 16
AFP, AFM = 18, 19
MK = 20
ST = 23
SW = 26
ZP, ZM, ZFP, ZFM = 28, 30, 32, 33
YP, YM = 34, 42
YFP, YFM = 50, 54
DO = 58
DYM, DYP, DYO = 66, 68, 70
OUT = 72
TOK = 76
COUNT = 77
AHEAD = 64
BYX = 64


def kernel(
    tok, bm, gn, wq, wk, wv, qg, kg, out, tv, nv, st, sg, a_buf, b_buf, acc, mk, mbuf, obuf, ssem, rsem
):
    dp = lax.axis_index("dp")
    t = lax.axis_index("tensor")
    x, y, zh = dp // 16, (dp // 4) % 4, dp % 4
    zlo, c = t // 2, t % 2
    xp, xm, xo = (x + 1) % 4, (x + 3) % 4, (x + 2) % 4
    yp, ym, yo = (y + 1) % 4, (y + 3) % 4, (y + 2) % 4
    zp, zm, zo = (zh + 1) % 4, (zh + 3) % 4, (zh + 2) % 4

    def dev(x_=None, y_=None, zh_=None, zlo_=None, c_=None):
        x_ = x if x_ is None else x_
        y_ = y if y_ is None else y_
        zh_ = zh if zh_ is None else zh_
        zlo_ = zlo if zlo_ is None else zlo_
        c_ = c if c_ is None else c_
        return (x_ * 16 + y_ * 4 + zh_, zlo_ * 2 + c_)

    def remote(src, dst, sid, rid, device):
        return pltpu.make_async_remote_copy(
            src_ref=src, dst_ref=dst, send_sem=ssem.at[sid], recv_sem=rsem.at[rid], device_id=device, device_id_type=MESH
        )

    def a_at(xb, q, r0=0, rows=TPD):
        return a_buf.at[pl.ds(pl.multiple_of(xb * TPD + r0, 64), rows), pl.ds(pl.multiple_of(q * FEAT, FEAT), FEAT)]

    def b_at(xw, yw, zw, n=1):
        return b_buf.at[pl.ds(pl.multiple_of(((xw * 4 + yw) * 4 + zw) * ROWS, ROWS), n * ROWS), :]

    def got(ref, rid):
        remote(ref, ref, 0, rid, dev(c_=1 - c)).wait_recv()

    def sent(ref, sid):
        remote(ref, ref, sid, 0, dev(c_=1 - c)).wait_send()

    def relay(ref, num, device):
        remote(ref, ref, num, num, device).start()

    load = pltpu.make_async_copy(tok, tv, rsem.at[TOK])
    load.start()

    barrier = pltpu.get_barrier_semaphore()
    for dx in range(4):
        for dc in range(2):
            if dx or dc:
                pl.semaphore_signal(barrier, inc=1, device_id=dev(x_=(x + dx) % 4, c_=(c + dc) % 2), device_id_type=MESH)
    for core in range(2):
        pl.semaphore_signal(barrier, inc=1, device_id=dev(zlo_=1 - zlo, c_=core), device_id_type=MESH)
    for other in (dev(y_=yp), dev(y_=ym), dev(zh_=zp), dev(zh_=zm)):
        pl.semaphore_signal(barrier, inc=1, device_id=other, device_id_type=MESH)

    kb = lax.broadcasted_iota(jnp.int32, (4, TPD), 1) // BLOCK
    qb = lax.broadcasted_iota(jnp.int32, (4, TPD), 0)
    for r in range(2):
        m = bm[r]
        seen = jnp.where(kb == 0, m[:, 0:1], jnp.where(kb == 1, m[:, 1:2], jnp.where(kb == 2, m[:, 2:3], m[:, 3:4])))
        mk[8 * r : 8 * r + 4, :] = jnp.where(jnp.logical_or(seen > 0, kb == qb), 1.0, 0.0)
        mk[8 * r + 4 : 8 * r + 8, :] = jnp.zeros((4, TPD), jnp.float32)
    mbuf[x] = mk[...]

    load.wait()
    lane = lax.broadcasted_iota(jnp.int32, (64, 128), 1)

    def stats(i, _):
        rr = pl.multiple_of(i * 64, 64)
        t1 = jnp.zeros((64, 128), jnp.float32)
        t2 = jnp.zeros((64, 128), jnp.float32)
        for j in range(FEAT // 128):
            v = tv[pl.ds(rr, 64), j * 128 : (j + 1) * 128].astype(jnp.float32)
            t1 = t1 + v
            t2 = t2 + v * v
        a1 = jnp.sum(t1, axis=-1, keepdims=True)
        a2 = jnp.sum(t2, axis=-1, keepdims=True)
        st[pl.ds(rr, 64), :] = jnp.where(lane == 0, a1, jnp.where(lane == 1, a2, 0.0))
        return 0

    lax.fori_loop(0, 8, stats, 0)
    for i in range(4):
        sg[t, :, i * 128 : (i + 1) * 128] = jnp.transpose(st[i * 128 : (i + 1) * 128, :])[:8]

    pl.semaphore_wait(barrier, 13)

    def swap(e, p, w):
        src = w.at[:, pl.ds(e * NC, NC)]
        here = b_at(x, y, zh).at[:, pl.ds(p * NC, NC)]
        away = jnp.logical_or(c + 2 * e != x, x // 2 != c)
        far = remote(src, here, SW + e, SW + x % 2, dev(x_=c + 2 * e, c_=x // 2))
        return away, far, pltpu.make_async_copy(src, here, rsem.at[SW + x % 2])

    for e in range(2):
        for p, w in enumerate((wq, wk, wv)):
            away, far, near = swap(e, p, w)

            @pl.when(away)
            def _():
                far.start()

            @pl.when(jnp.logical_not(away))
            def _():
                near.start()

    peers = [dev(c_=1 - c), dev(zlo_=1 - zlo), dev(zlo_=1 - zlo, c_=1 - c)]
    for k in range(3):
        remote(sg.at[t], sg.at[t], ST + k, ST + k, peers[k]).start()
    for k in range(3):
        remote(mk, mbuf.at[x], MK + k, MK + k, dev(x_=(x + k + 1) % 4)).start()
    theirs = [t + 1 - 2 * c, (t + 2) % 4, (t + 2) % 4 + 1 - 2 * c]
    for k in range(3):
        got(sg.at[theirs[k]], ST + k)
    total = (sg[0] + sg[1]) + (sg[2] + sg[3])
    mean = total[0:1] * (1.0 / D)
    rstd = lax.rsqrt(total[1:2] * (1.0 / D) - mean * mean + EPS)
    row = lax.broadcasted_iota(jnp.int32, (128, 128), 0)
    for i in range(4):
        cols = slice(i * 128, (i + 1) * 128)
        st[i * 128 : (i + 1) * 128, :] = jnp.transpose(jnp.where(row == 0, mean[:, cols], rstd[:, cols]))

    def norm(i, _):
        rr = pl.multiple_of(i * 64, 64)
        mu = jnp.broadcast_to(st[pl.ds(rr, 64), 0:1], (64, 128))
        rs = jnp.broadcast_to(st[pl.ds(rr, 64), 1:2], (64, 128))
        for j in range(FEAT // 128):
            v = tv[pl.ds(rr, 64), j * 128 : (j + 1) * 128].astype(jnp.float32)
            g = gn[:, pl.ds(pl.multiple_of(t * FEAT + j * 128, 128), 128)]
            nv[pl.ds(rr, 64), j * 128 : (j + 1) * 128] = ((v - mu) * rs * g).astype(jnp.bfloat16)
        return 0

    lax.fori_loop(0, 8, norm, 0)

    def first(r, dst_dev, base, r0=0, rows=TPD):
        return remote(nv.at[pl.ds(r * TPD + r0, rows), :], a_at(x, t, r0, rows), base + r, base + c, dst_dev)

    def pair(r, r0, rows, base):
        return first(r, dev(zlo_=1 - zlo, c_=r), base, r0, rows)

    for r in range(2):
        first(r, dev(x_=xp, c_=r), AXP).start()
        first(r, dev(x_=xm, c_=r), AXM).start()
        pair(r, 0, AHEAD, AZ).start()
    half = nv.at[pl.ds(pl.multiple_of((1 - c) * TPD, TPD), TPD), :]
    remote(half, a_at(x, t), AD, AD, dev(c_=1 - c)).start()
    own = pltpu.make_async_copy(nv.at[pl.ds(pl.multiple_of(c * TPD, TPD), TPD), :], a_at(x, t), rsem.at[AL])
    own.start()

    xw = [2 * c, 2 * c + 1]
    names = [zh, zm, zp, zo]

    def y_out(k, h):
        piece = b_at(xw[h], y, names[k])
        relay(piece, YP + 2 * k + h, dev(y_=yp))
        relay(piece, YM + 2 * k + h, dev(y_=ym))
        relay(piece, DO + 2 * k + h, dev(c_=1 - c))

    def y_on(k, h):
        got(b_at(xw[h], ym, names[k]), YP + 2 * k + h)
        if h == 0:
            relay(b_at(xw[0], ym, names[k]), YFP + k, dev(y_=yp))
        got(b_at(xw[h], yp, names[k]), YM + 2 * k + h)
        if h == 1:
            relay(b_at(xw[1], yp, names[k]), YFM + k, dev(y_=ym))

    for h in range(2):
        piece = b_at(xw[h], y, zh)
        got(piece, SW + h)
        relay(piece, ZP + h, dev(zh_=zp))
        relay(piece, ZM + h, dev(zh_=zm))
        y_out(0, h)

    acc[...] = jnp.zeros_like(acc)
    y_on(0, 0)
    got(b_at(xw[0], y, zm), ZP)
    relay(b_at(xw[0], y, zm), ZFP, dev(zh_=zp))
    y_out(1, 0)
    got(b_at(xw[0], y, zp), ZM)
    y_out(2, 0)
    y_on(0, 1)
    got(b_at(xw[1], y, zm), ZP + 1)
    y_out(1, 1)
    got(b_at(xw[1], y, zp), ZM + 1)
    relay(b_at(xw[1], y, zp), ZFM, dev(zh_=zm))
    y_out(2, 1)
    for r in range(2):
        pair(r, AHEAD, TPD - AHEAD, AZL).start()
    y_on(1, 0)
    y_on(2, 0)
    got(b_at(xw[0], y, zo), ZFP)
    y_out(3, 0)
    got(b_at(xw[1], y, zo), ZFM)
    y_out(3, 1)
    y_on(1, 1)
    for q in range(2):
        got(a_at(xm, 2 * zlo + q), AXP + q)
        got(a_at(xp, 2 * zlo + q), AXM + q)
        if q == 0:
            relay(a_at(xm, 2 * zlo), AOP, dev(x_=xp))
    relay(a_at(xp, 2 * zlo + 1), AOM, dev(x_=xm))
    y_on(2, 1)
    y_on(3, 0)
    y_on(3, 1)
    for base, yy in ((DYM, ym), (DYP, yp)):
        for h in range(2):
            relay(b_at(xw[h], yy, 0, 4), base + h, dev(c_=1 - c))
    for q in range(2):
        got(a_at(x, 2 * (1 - zlo) + q, 0, AHEAD), AZ + q)
        got(a_at(x, 2 * (1 - zlo) + q, AHEAD, TPD - AHEAD), AZL + q)
        piece = a_at(x, 2 * (1 - zlo) + q)
        relay(piece, AIIP + q, dev(x_=xp))
        relay(piece, AIIM + q, dev(x_=xm))
    got(a_at(xo, 2 * zlo), AOP)
    relay(a_at(xo, 2 * zlo), AIII, dev(zlo_=1 - zlo))
    got(a_at(xo, 2 * zlo + 1), AOM)
    relay(a_at(xo, 2 * zlo + 1, 0, TPD - 2 * BYX), AIII + 1, dev(zlo_=1 - zlo))
    for k in range(4):
        got(b_at(xw[0], yo, names[k]), YFP + k)
        got(b_at(xw[1], yo, names[k]), YFM + k)
    for h in range(2):
        relay(b_at(xw[h], yo, 0, 4), DYO + h, dev(c_=1 - c))
    xv = [2 * (1 - c), 2 * (1 - c) + 1]
    for h in range(2):
        for k in range(4):
            got(b_at(xv[h], y, names[k]), DO + 2 * k + h)
    for base, yy in ((DYM, ym), (DYP, yp), (DYO, yo)):
        for h in range(2):
            got(b_at(xv[h], yy, 0, 4), base + h)
    got(a_at(x, 2 * zlo + 1 - c), AD)
    own.wait()
    for k in range(3):
        got(mbuf.at[(x + 3 - k) % 4], MK + k)

    def unit(xb, q):
        row = pl.multiple_of(xb * TPD, TPD)
        col = pl.multiple_of(q * FEAT, FEAT)
        acc[pl.ds(row, TPD), :] += jnp.dot(
            a_buf[pl.ds(row, TPD), pl.ds(col, FEAT)], b_buf[pl.ds(col, FEAT), :], preferred_element_type=jnp.float32
        )

    def order(i):
        return (x + jnp.where(i == 1, 3, jnp.where(i == 2, 1, jnp.where(i == 3, 2, 0)))) % 4

    def near(i, _):
        b = jnp.where(i < 4, 0, i // 2 - 1)
        q = jnp.where(i < 4, i % 4, i % 2)
        unit(order(b), (2 * zlo + q) % 4)
        return 0

    lax.fori_loop(0, 10, near, 0)

    def out_copy(xb, i):
        src = obuf.at[i]
        dst = out.at[pl.ds(pl.multiple_of(c * TPD, TPD), TPD), pl.ds(pl.multiple_of((x // 2) * NC, NC), NC)]
        rid = OUT + 2 * (x // 2) + c
        away = jnp.logical_or(xb != x, x % 2 != c)
        return away, remote(src, dst, OUT + i, rid, dev(x_=xb, c_=x % 2)), pltpu.make_async_copy(src, dst, rsem.at[rid])

    def finish(i):
        xb = order(i)
        row = pl.multiple_of(xb * TPD, TPD)

        def part(p, j):
            return acc[pl.ds(row, TPD), p * NC + j * DH : p * NC + (j + 1) * DH]

        def head_norm(values, gain):
            ms = jnp.mean(values * values, axis=-1, keepdims=True)
            return (values * lax.rsqrt(ms + EPS) * gain).astype(jnp.bfloat16)

        allowed = mbuf[xb]
        seen = jnp.concatenate(
            [jnp.broadcast_to(jnp.where(c == 0, allowed[b : b + 1], allowed[8 + b : 9 + b]), (BLOCK, TPD)) for b in range(4)], axis=0
        )
        for j in range(3):
            qn = head_norm(part(0, j), qg[...])
            kn = head_norm(part(1, j), kg[...])
            v = part(2, j).astype(jnp.bfloat16)
            s = lax.dot_general(qn, kn, (((1,), (1,)), ((), ())), preferred_element_type=jnp.float32) * (1.0 / DH**0.5)
            s = jnp.where(seen > 0, s, jnp.float32(-1e30))
            w = jnp.exp(s - jnp.max(s, axis=-1, keepdims=True))
            probs = (w / jnp.sum(w, axis=-1, keepdims=True)).astype(jnp.bfloat16)
            obuf[i, :, j * DH : (j + 1) * DH] = jnp.dot(probs, v, preferred_element_type=jnp.float32).astype(jnp.bfloat16)
        away, far, near_ = out_copy(xb, i)

        @pl.when(away)
        def _():
            far.start()

        @pl.when(jnp.logical_not(away))
        def _():
            near_.start()

    finish(0)

    def third(i, _):
        for k, (num, blk) in enumerate(((AIIP, xm), (AIIM, xp), (AIII, xo))):

            @pl.when(i == k + 1)
            def _():
                got(a_at(blk, 2 * (1 - zlo)), num)

        unit(order(i), 2 * (1 - zlo))
        return 0

    lax.fori_loop(1, 4, third, 0)
    far_q = 2 * (1 - zlo) + 1
    got(a_at(xm, far_q), AIIP + 1)
    relay(a_at(xm, far_q, TPD - 2 * BYX, BYX), AFP, dev(x_=xp))
    got(a_at(xp, far_q), AIIM + 1)
    relay(a_at(xp, far_q, TPD - BYX, BYX), AFM, dev(x_=xm))

    def last(i, _):
        @pl.when(i == 3)
        def _():
            got(a_at(xo, far_q, 0, TPD - 2 * BYX), AIII + 1)
            got(a_at(xo, far_q, TPD - 2 * BYX, BYX), AFP)
            got(a_at(xo, far_q, TPD - BYX, BYX), AFM)

        unit(order(i), far_q)
        finish(i)
        return 0

    lax.fori_loop(1, 4, last, 0)

    for e in range(2):
        for r in range(2):
            got(out.at[pl.ds(r * TPD, TPD), pl.ds(e * NC, NC)], OUT + 2 * e + r)
    for num in (AXP, AXP + 1, AXM, AXM + 1, AD, AOP, AOM, AIIP, AIIP + 1, AIIM, AIIM + 1, AIII):
        sent(a_at(x, t), num)
    sent(a_at(x, t, 0, TPD - 2 * BYX), AIII + 1)
    for r in range(2):
        sent(a_at(x, t, 0, AHEAD), AZ + r)
        sent(a_at(x, t, AHEAD, TPD - AHEAD), AZL + r)
    for num in (AFP, AFM):
        sent(a_at(x, t, 0, BYX), num)
    for k in range(3):
        sent(mk, MK + k)
        sent(sg.at[t], ST + k)
    for e in range(2):

        @pl.when(jnp.logical_or(c + 2 * e != x, x // 2 != c))
        def _():
            sent(b_at(x, y, zh), SW + e)

    for num in range(ZP, DYM):
        sent(b_at(x, y, zh), num)
    for num in range(DYM, OUT):
        sent(b_at(x, y, 0, 4), num)
    for i in range(4):
        away, far, _ = out_copy(order(i), i)

        @pl.when(away)
        def _():
            far.wait_send()


def per_device(tokens, block_mask, norm_gain, w_query, w_key, w_value, query_gain, key_gain):
    vmem = pl.BlockSpec(memory_space=pltpu.VMEM)
    hbm = pl.BlockSpec(memory_space=pl.ANY)
    return pl.pallas_call(
        kernel,
        out_shape=jax.ShapeDtypeStruct((512, 768), jnp.bfloat16),
        in_specs=[hbm, vmem, vmem, hbm, hbm, hbm, vmem, vmem],
        out_specs=hbm,
        scratch_shapes=[
            pltpu.VMEM((2 * TPD, FEAT), jnp.bfloat16),
            pltpu.VMEM((2 * TPD, FEAT), jnp.bfloat16),
            pltpu.VMEM((2 * TPD, 128), jnp.float32),
            pltpu.VMEM((4, 8, 2 * TPD), jnp.float32),
            pltpu.VMEM((4 * TPD, D), jnp.bfloat16),
            pltpu.VMEM((D, N), jnp.bfloat16),
            pltpu.VMEM((4 * TPD, N), jnp.float32),
            pltpu.VMEM((16, TPD), jnp.float32),
            pltpu.VMEM((4, 16, TPD), jnp.float32),
            pltpu.VMEM((4, TPD, NC), jnp.bfloat16),
            pltpu.SemaphoreType.DMA((COUNT,)),
            pltpu.SemaphoreType.DMA((COUNT,)),
        ],
        compiler_params=pltpu.CompilerParams(collective_id=0, has_side_effects=True, vmem_limit_bytes=60 << 20),
    )(tokens, block_mask, norm_gain.reshape(1, D), w_query, w_key, w_value, query_gain.reshape(1, DH), key_gain.reshape(1, DH))


def solution(mesh):
    return jax.shard_map(
        per_device,
        mesh=mesh,
        in_specs=(
            P("dp", "tensor"),
            P("dp", None, None),
            P(),
            P("dp", "tensor"),
            P("dp", "tensor"),
            P("dp", "tensor"),
            P(),
            P(),
        ),
        out_specs=P("dp", "tensor"),
        check_vma=False,
    )
```

time: 135 us -> 138 us (1.022)
  Pallas kernels: 128 us -> 133 us
  local copies, waits for them, and re-layouts: 4.3 us -> 2.06 us
    pallas_call x1, Pallas kernels: 128 us -> 133 us  [per_device(): pl.pallas_call(kernel, out_shape=jax.ShapeDtypeStruct((512, 768), jnp.bfl...]
where the time goes in v2:
time: 138 us; the launch traced here: 135 us
  Pallas kernels  133 us (96%)
  local copies, waits for them, and re-layouts  2.06 us (1%)
    pallas_call x1, Pallas kernels, per_device(): pl.pallas_call(kernel, out_shape=jax.ShapeDtypeStruct((512, 768), jnp.bfl...  133 us

profile of v2, /device:TPU:1, one launch (start us, length us, event | category | flops | bytes accessed | tf_op | source)
XLA Modules:
  0.0 135.3 jit_solution(2994347186092632326)
XLA Ops:
  0.0 133.2 %shard_map.82 = bf16[512,768]{1,0:T(8,128)(2,1)} custom-call(bf16[512,1536]{1,0:T(8,128)(2,1)} %tok.1, s32[2,4,4]{2,1,0:T(4,128)} %bm.1, f32[1,6144]{1,0:T(1,128)} %bitcast.3, bf16[96,768]{1,0:T(8,128)(2,1)} %wq.1, bf16[96,768]{1,0:T(8,128)(2,1)} %wk.1, bf16[96,768]{1,0:T(8,128)(2,1)} %wv.1, f32[1,128]{1,0:T(1,128)} %bitcast.4, f32[1,128]{1,0:T(1,128)} %bitcast.5), custom_call_target="tpu_custom_call" | custom-call | tf_op jit(solution)/shard_map/pallas_call | solution.py:395
  133.2 2.1 %copy.10 = bf16[512,768]{1,0:T(8,128)(2,1)} copy(bf16[512,768]{1,0:T(8,128)(2,1)} %shard_map.82) | data formatting | bytes 1572864

commit v3 on v2

--- a/solution.py
+++ b/solution.py
@@ -17,7 +17,7 @@
 NC = 384
 N = 3 * NC
 
-AXP, AXM, AZ, AZL = 0, 2, 4, 6
+AXP, AXM, AZ = 0, 2, 4
 AD, AL, AOP, AOM = 8, 9, 10, 11
 AIIP, AIIM, AIII = 12, 14, 16
 AFP, AFM = 18, 19
@@ -32,7 +32,6 @@
 OUT = 72
 TOK = 76
 COUNT = 77
-AHEAD = 64
 BYX = 64
 
 
@@ -166,16 +165,13 @@
 
     lax.fori_loop(0, 8, norm, 0)
 
-    def first(r, dst_dev, base, r0=0, rows=TPD):
-        return remote(nv.at[pl.ds(r * TPD + r0, rows), :], a_at(x, t, r0, rows), base + r, base + c, dst_dev)
-
-    def pair(r, r0, rows, base):
-        return first(r, dev(zlo_=1 - zlo, c_=r), base, r0, rows)
-
-    for r in range(2):
+    def first(r, dst_dev, base):
+        return remote(nv.at[pl.ds(pl.multiple_of(r * TPD, TPD), TPD), :], a_at(x, t), base + r, base + c, dst_dev)
+
+    turns = [c, 1 - c]
+    for r in turns:
         first(r, dev(x_=xp, c_=r), AXP).start()
         first(r, dev(x_=xm, c_=r), AXM).start()
-        pair(r, 0, AHEAD, AZ).start()
     half = nv.at[pl.ds(pl.multiple_of((1 - c) * TPD, TPD), TPD), :]
     remote(half, a_at(x, t), AD, AD, dev(c_=1 - c)).start()
     own = pltpu.make_async_copy(nv.at[pl.ds(pl.multiple_of(c * TPD, TPD), TPD), :], a_at(x, t), rsem.at[AL])
@@ -206,6 +202,13 @@
         y_out(0, h)
 
     acc[...] = jnp.zeros_like(acc)
+
+    def pair_on(q):
+        piece = a_at(x, 2 * (1 - zlo) + q)
+        got(piece, AZ + q)
+        relay(piece, AIIP + q, dev(x_=xp))
+        relay(piece, AIIM + q, dev(x_=xm))
+
     y_on(0, 0)
     got(b_at(xw[0], y, zm), ZP)
     relay(b_at(xw[0], y, zm), ZFP, dev(zh_=zp))
@@ -218,8 +221,8 @@
     got(b_at(xw[1], y, zp), ZM + 1)
     relay(b_at(xw[1], y, zp), ZFM, dev(zh_=zm))
     y_out(2, 1)
-    for r in range(2):
-        pair(r, AHEAD, TPD - AHEAD, AZL).start()
+    for r in turns:
+        first(r, dev(zlo_=1 - zlo, c_=r), AZ).start()
     y_on(1, 0)
     y_on(2, 0)
     got(b_at(xw[0], y, zo), ZFP)
@@ -227,24 +230,20 @@
     got(b_at(xw[1], y, zo), ZFM)
     y_out(3, 1)
     y_on(1, 1)
-    for q in range(2):
-        got(a_at(xm, 2 * zlo + q), AXP + q)
-        got(a_at(xp, 2 * zlo + q), AXM + q)
-        if q == 0:
-            relay(a_at(xm, 2 * zlo), AOP, dev(x_=xp))
+    got(a_at(xm, 2 * zlo), AXP)
+    relay(a_at(xm, 2 * zlo), AOP, dev(x_=xp))
+    got(a_at(xp, 2 * zlo + 1), AXM + 1)
     relay(a_at(xp, 2 * zlo + 1), AOM, dev(x_=xm))
     y_on(2, 1)
+    pair_on(c)
     y_on(3, 0)
     y_on(3, 1)
     for base, yy in ((DYM, ym), (DYP, yp)):
         for h in range(2):
             relay(b_at(xw[h], yy, 0, 4), base + h, dev(c_=1 - c))
-    for q in range(2):
-        got(a_at(x, 2 * (1 - zlo) + q, 0, AHEAD), AZ + q)
-        got(a_at(x, 2 * (1 - zlo) + q, AHEAD, TPD - AHEAD), AZL + q)
-        piece = a_at(x, 2 * (1 - zlo) + q)
-        relay(piece, AIIP + q, dev(x_=xp))
-        relay(piece, AIIM + q, dev(x_=xm))
+    pair_on(1 - c)
+    got(a_at(xm, 2 * zlo + 1), AXP + 1)
+    got(a_at(xp, 2 * zlo), AXM)
     got(a_at(xo, 2 * zlo), AOP)
     relay(a_at(xo, 2 * zlo), AIII, dev(zlo_=1 - zlo))
     got(a_at(xo, 2 * zlo + 1), AOM)
@@ -364,8 +363,7 @@
         sent(a_at(x, t), num)
     sent(a_at(x, t, 0, TPD - 2 * BYX), AIII + 1)
     for r in range(2):
-        sent(a_at(x, t, 0, AHEAD), AZ + r)
-        sent(a_at(x, t, AHEAD, TPD - AHEAD), AZL + r)
+        sent(a_at(x, t), AZ + r)
     for num in (AFP, AFM):
         sent(a_at(x, t, 0, BYX), num)
     for k in range(3):

time: 138 us -> 123 us (0.89)
  the two profiles are of different devices: /device:TPU:1 before, /device:TPU:32 now
where the time goes in v3:
time: 123 us
  Pallas kernels  121 us (98%)
  local copies, waits for them, and re-layouts  2.06 us (2%)
    pallas_call x1, Pallas kernels, per_device(): pl.pallas_call(kernel, out_shape=jax.ShapeDtypeStruct((512, 768), jnp.bfl...  121 us

profile of v3, /device:TPU:32, one launch (start us, length us, event | category | flops | bytes accessed | tf_op | source)
XLA Modules:
  0.0 123.3 jit_solution(7972813154894233586)
XLA Ops:
  0.0 121.2 %shard_map.82 = bf16[512,768]{1,0:T(8,128)(2,1)} custom-call(bf16[512,1536]{1,0:T(8,128)(2,1)} %tok.1, s32[2,4,4]{2,1,0:T(4,128)} %bm.1, f32[1,6144]{1,0:T(1,128)} %bitcast.3, bf16[96,768]{1,0:T(8,128)(2,1)} %wq.1, bf16[96,768]{1,0:T(8,128)(2,1)} %wk.1, bf16[96,768]{1,0:T(8,128)(2,1)} %wv.1, f32[1,128]{1,0:T(1,128)} %bitcast.4, f32[1,128]{1,0:T(1,128)} %bitcast.5), custom_call_target="tpu_custom_call" | custom-call | tf_op jit(solution)/shard_map/pallas_call | solution.py:393
  121.2 2.1 %copy.10 = bf16[512,768]{1,0:T(8,128)(2,1)} copy(bf16[512,768]{1,0:T(8,128)(2,1)} %shard_map.82) | data formatting | bytes 1572864

commit v4 on v3

--- a/solution.py
+++ b/solution.py
@@ -31,8 +31,10 @@
 DYM, DYP, DYO = 66, 68, 70
 OUT = 72
 TOK = 76
-COUNT = 77
-BYX = 64
+ALP, ALM = 77, 78
+AQP, AQM, AIV = 79, 80, 81
+COUNT = 82
+BYX = 96
 
 
 def kernel(
@@ -60,7 +62,7 @@
         )
 
     def a_at(xb, q, r0=0, rows=TPD):
-        return a_buf.at[pl.ds(pl.multiple_of(xb * TPD + r0, 64), rows), pl.ds(pl.multiple_of(q * FEAT, FEAT), FEAT)]
+        return a_buf.at[pl.ds(pl.multiple_of(xb * TPD + r0, 16), rows), pl.ds(pl.multiple_of(q * FEAT, FEAT), FEAT)]
 
     def b_at(xw, yw, zw, n=1):
         return b_buf.at[pl.ds(pl.multiple_of(((xw * 4 + yw) * 4 + zw) * ROWS, ROWS), n * ROWS), :]
@@ -95,6 +97,27 @@
         mk[8 * r : 8 * r + 4, :] = jnp.where(jnp.logical_or(seen > 0, kb == qb), 1.0, 0.0)
         mk[8 * r + 4 : 8 * r + 8, :] = jnp.zeros((4, TPD), jnp.float32)
     mbuf[x] = mk[...]
+
+    pl.semaphore_wait(barrier, 13)
+
+    def swap(e, p, w):
+        src = w.at[:, pl.ds(e * NC, NC)]
+        here = b_at(x, y, zh).at[:, pl.ds(p * NC, NC)]
+        away = jnp.logical_or(c + 2 * e != x, x // 2 != c)
+        far = remote(src, here, SW + e, SW + x % 2, dev(x_=c + 2 * e, c_=x // 2))
+        return away, far, pltpu.make_async_copy(src, here, rsem.at[SW + x % 2])
+
+    for e in range(2):
+        for p, w in enumerate((wq, wk, wv)):
+            away, far, near = swap(e, p, w)
+
+            @pl.when(away)
+            def _():
+                far.start()
+
+            @pl.when(jnp.logical_not(away))
+            def _():
+                near.start()
 
     load.wait()
     lane = lax.broadcasted_iota(jnp.int32, (64, 128), 1)
@@ -115,27 +138,6 @@
     lax.fori_loop(0, 8, stats, 0)
     for i in range(4):
         sg[t, :, i * 128 : (i + 1) * 128] = jnp.transpose(st[i * 128 : (i + 1) * 128, :])[:8]
-
-    pl.semaphore_wait(barrier, 13)
-
-    def swap(e, p, w):
-        src = w.at[:, pl.ds(e * NC, NC)]
-        here = b_at(x, y, zh).at[:, pl.ds(p * NC, NC)]
-        away = jnp.logical_or(c + 2 * e != x, x // 2 != c)
-        far = remote(src, here, SW + e, SW + x % 2, dev(x_=c + 2 * e, c_=x // 2))
-        return away, far, pltpu.make_async_copy(src, here, rsem.at[SW + x % 2])
-
-    for e in range(2):
-        for p, w in enumerate((wq, wk, wv)):
-            away, far, near = swap(e, p, w)
-
-            @pl.when(away)
-            def _():
-                far.start()
-
-            @pl.when(jnp.logical_not(away))
-            def _():
-                near.start()
 
     peers = [dev(c_=1 - c), dev(zlo_=1 - zlo), dev(zlo_=1 - zlo, c_=1 - c)]
     for k in range(3):
@@ -163,13 +165,12 @@
             nv[pl.ds(rr, 64), j * 128 : (j + 1) * 128] = ((v - mu) * rs * g).astype(jnp.bfloat16)
         return 0
 
-    lax.fori_loop(0, 8, norm, 0)
-
     def first(r, dst_dev, base):
         return remote(nv.at[pl.ds(pl.multiple_of(r * TPD, TPD), TPD), :], a_at(x, t), base + r, base + c, dst_dev)
 
     turns = [c, 1 - c]
     for r in turns:
+        lax.fori_loop(r * 4, r * 4 + 4, norm, 0)
         first(r, dev(x_=xp, c_=r), AXP).start()
         first(r, dev(x_=xm, c_=r), AXM).start()
     half = nv.at[pl.ds(pl.multiple_of((1 - c) * TPD, TPD), TPD), :]
@@ -203,12 +204,51 @@
 
     acc[...] = jnp.zeros_like(acc)
 
-    def pair_on(q):
-        piece = a_at(x, 2 * (1 - zlo) + q)
-        got(piece, AZ + q)
-        relay(piece, AIIP + q, dev(x_=xp))
-        relay(piece, AIIM + q, dev(x_=xm))
-
+    near_q = [2 * zlo + c, 2 * zlo + 1 - c]
+    far_q = [2 * (1 - zlo) + c, 2 * (1 - zlo) + 1 - c]
+    MID = TPD // 2
+
+    def pair_on(part, plus, minus, r0, rows):
+        piece = a_at(x, far_q[part], r0, rows)
+        relay(piece, plus, dev(x_=xp))
+        relay(piece, minus, dev(x_=xm))
+
+    def order(i):
+        return (x + jnp.where(i == 1, 3, jnp.where(i == 2, 1, jnp.where(i == 3, 2, 0)))) % 4
+
+    def chunk(xb, half, yy):
+        row = pl.multiple_of(xb * TPD, TPD)
+        at = [pl.ds(pl.multiple_of(((2 * half + k) * 4 + yy) * 4 * ROWS, 128), 4 * ROWS) for k in range(2)]
+        acc[pl.ds(row, TPD), :] += jnp.dot(
+            jnp.concatenate([a_buf[pl.ds(row, TPD), at[k]] for k in range(2)], axis=1),
+            jnp.concatenate([b_buf[at[k], :] for k in range(2)], axis=0),
+            preferred_element_type=jnp.float32,
+        )
+
+    def beside(i):
+        return (y + jnp.where(i == 1, 3, jnp.where(i == 2, 1, 0))) % 4
+
+    def early(i, _):
+        chunk(order(i), zlo, y)
+        return 0
+
+    def middle(i, _):
+        chunk(order(i // 2), zlo, beside(1 + i % 2))
+        return 0
+
+    def opposite(i, _):
+        chunk(xo, zlo, beside(i))
+        return 0
+
+    def across(i, _):
+        chunk(x, 1 - zlo, beside(i))
+        return 0
+
+    def late(i, _):
+        chunk(order(jnp.where(i == 4, 0, i)), jnp.where(i == 4, 1 - zlo, zlo), yo)
+        return 0
+
+    xv = [2 * (1 - c), 2 * (1 - c) + 1]
     y_on(0, 0)
     got(b_at(xw[0], y, zm), ZP)
     relay(b_at(xw[0], y, zm), ZFP, dev(zh_=zp))
@@ -221,74 +261,83 @@
     got(b_at(xw[1], y, zp), ZM + 1)
     relay(b_at(xw[1], y, zp), ZFM, dev(zh_=zm))
     y_out(2, 1)
-    for r in turns:
-        first(r, dev(zlo_=1 - zlo, c_=r), AZ).start()
     y_on(1, 0)
     y_on(2, 0)
     got(b_at(xw[0], y, zo), ZFP)
+    for r in turns:
+        first(r, dev(zlo_=1 - zlo, c_=r), AZ).start()
     y_out(3, 0)
     got(b_at(xw[1], y, zo), ZFM)
     y_out(3, 1)
+    def ahead(part, plus, minus, core):
+        got(a_at(xm, near_q[part]), AXP + core)
+        relay(a_at(xm, near_q[part], 0, MID), plus, dev(x_=xp))
+        got(a_at(xp, near_q[part]), AXM + core)
+        relay(a_at(xp, near_q[part], MID, MID), minus, dev(x_=xm))
+
+    ahead(0, AOP, AOM, c)
     y_on(1, 1)
-    got(a_at(xm, 2 * zlo), AXP)
-    relay(a_at(xm, 2 * zlo), AOP, dev(x_=xp))
-    got(a_at(xp, 2 * zlo + 1), AXM + 1)
-    relay(a_at(xp, 2 * zlo + 1), AOM, dev(x_=xm))
     y_on(2, 1)
-    pair_on(c)
+    ahead(1, AQP, AQM, 1 - c)
+    for h in range(2):
+        for k in range(4):
+            got(b_at(xv[h], y, names[k]), DO + 2 * k + h)
+    got(a_at(x, 2 * zlo + 1 - c), AD)
+    own.wait()
+    lax.fori_loop(0, 3, early, 0)
+    got(a_at(x, far_q[0]), AZ + c)
+    pair_on(0, AIIP, AIIM, 0, TPD)
     y_on(3, 0)
     y_on(3, 1)
     for base, yy in ((DYM, ym), (DYP, yp)):
         for h in range(2):
             relay(b_at(xw[h], yy, 0, 4), base + h, dev(c_=1 - c))
-    pair_on(1 - c)
-    got(a_at(xm, 2 * zlo + 1), AXP + 1)
-    got(a_at(xp, 2 * zlo), AXM)
-    got(a_at(xo, 2 * zlo), AOP)
-    relay(a_at(xo, 2 * zlo), AIII, dev(zlo_=1 - zlo))
-    got(a_at(xo, 2 * zlo + 1), AOM)
-    relay(a_at(xo, 2 * zlo + 1, 0, TPD - 2 * BYX), AIII + 1, dev(zlo_=1 - zlo))
-    for k in range(4):
-        got(b_at(xw[0], yo, names[k]), YFP + k)
-        got(b_at(xw[1], yo, names[k]), YFM + k)
-    for h in range(2):
-        relay(b_at(xw[h], yo, 0, 4), DYO + h, dev(c_=1 - c))
-    xv = [2 * (1 - c), 2 * (1 - c) + 1]
-    for h in range(2):
-        for k in range(4):
-            got(b_at(xv[h], y, names[k]), DO + 2 * k + h)
-    for base, yy in ((DYM, ym), (DYP, yp), (DYO, yo)):
+    got(a_at(xo, near_q[0], 0, MID), AOP)
+    relay(a_at(xo, near_q[0], 0, TPD - 2 * BYX), AIII, dev(zlo_=1 - zlo))
+    got(a_at(xo, near_q[1], 0, MID), AQP)
+    relay(a_at(xo, near_q[1], 0, MID), AIII + 1, dev(zlo_=1 - zlo))
+    got(a_at(xo, near_q[1], MID, MID), AQM)
+    relay(a_at(xo, near_q[1], MID, MID), AIV, dev(zlo_=1 - zlo))
+    for base, yy in ((DYM, ym), (DYP, yp)):
         for h in range(2):
             got(b_at(xv[h], yy, 0, 4), base + h)
-    got(a_at(x, 2 * zlo + 1 - c), AD)
-    own.wait()
+    lax.fori_loop(0, 6, middle, 0)
+    got(a_at(x, far_q[1]), AZ + 1 - c)
+    pair_on(1, AIIP + 1, AIIM + 1, 0, MID)
+    got(a_at(xo, near_q[0], MID, MID), AOM)
+    lax.fori_loop(0, 3, opposite, 0)
+    for h, num in enumerate((YFP, YFM)):
+        for k in range(4):
+            got(b_at(xw[h], yo, names[k]), num + k)
+        relay(b_at(xw[h], yo, 0, 4), DYO + h, dev(c_=1 - c))
+    got(a_at(xm, far_q[0]), AIIP)
+    relay(a_at(xm, far_q[0], TPD - 2 * BYX, BYX), AFP, dev(x_=xp))
+    got(a_at(xp, far_q[0]), AIIM)
+    relay(a_at(xp, far_q[0], TPD - BYX, BYX), AFM, dev(x_=xm))
+    pair_on(1, ALP, ALM, MID, MID)
+    lax.fori_loop(0, 3, across, 0)
+    for h in range(2):
+        got(b_at(xv[h], yo, 0, 4), DYO + h)
+    lax.fori_loop(0, 5, late, 0)
     for k in range(3):
         got(mbuf.at[(x + 3 - k) % 4], MK + k)
 
-    def unit(xb, q):
-        row = pl.multiple_of(xb * TPD, TPD)
+    def unit(xb, q, r0=0, n=TPD):
+        row = pl.multiple_of(xb * TPD + r0, MID)
         col = pl.multiple_of(q * FEAT, FEAT)
-        acc[pl.ds(row, TPD), :] += jnp.dot(
-            a_buf[pl.ds(row, TPD), pl.ds(col, FEAT)], b_buf[pl.ds(col, FEAT), :], preferred_element_type=jnp.float32
+        acc[pl.ds(row, n), :] += jnp.dot(
+            a_buf[pl.ds(row, n), pl.ds(col, FEAT)], b_buf[pl.ds(col, FEAT), :], preferred_element_type=jnp.float32
         )
 
-    def order(i):
-        return (x + jnp.where(i == 1, 3, jnp.where(i == 2, 1, jnp.where(i == 3, 2, 0)))) % 4
-
-    def near(i, _):
-        b = jnp.where(i < 4, 0, i // 2 - 1)
-        q = jnp.where(i < 4, i % 4, i % 2)
-        unit(order(b), (2 * zlo + q) % 4)
-        return 0
-
-    lax.fori_loop(0, 10, near, 0)
-
-    def out_copy(xb, i):
-        src = obuf.at[i]
-        dst = out.at[pl.ds(pl.multiple_of(c * TPD, TPD), TPD), pl.ds(pl.multiple_of((x // 2) * NC, NC), NC)]
+    def out_copy(xb, i, j):
+        src = obuf.at[i, :, pl.ds(j * DH, DH)]
+        cols = pl.ds(pl.multiple_of((x // 2) * NC + j * DH, DH), DH)
+        dst = out.at[pl.ds(pl.multiple_of(c * TPD, TPD), TPD), cols]
         rid = OUT + 2 * (x // 2) + c
-        away = jnp.logical_or(xb != x, x % 2 != c)
-        return away, remote(src, dst, OUT + i, rid, dev(x_=xb, c_=x % 2)), pltpu.make_async_copy(src, dst, rsem.at[rid])
+        return remote(src, dst, OUT + i, rid, dev(x_=xb, c_=x % 2)), pltpu.make_async_copy(src, dst, rsem.at[rid])
+
+    def goes(xb):
+        return jnp.logical_or(xb != x, x % 2 != c)
 
     def finish(i):
         xb = order(i)
@@ -314,54 +363,68 @@
             w = jnp.exp(s - jnp.max(s, axis=-1, keepdims=True))
             probs = (w / jnp.sum(w, axis=-1, keepdims=True)).astype(jnp.bfloat16)
             obuf[i, :, j * DH : (j + 1) * DH] = jnp.dot(probs, v, preferred_element_type=jnp.float32).astype(jnp.bfloat16)
-        away, far, near_ = out_copy(xb, i)
-
-        @pl.when(away)
-        def _():
-            far.start()
-
-        @pl.when(jnp.logical_not(away))
-        def _():
-            near_.start()
+            far, near_ = out_copy(xb, i, j)
+
+            @pl.when(goes(xb))
+            def _():
+                far.start()
+
+            @pl.when(jnp.logical_not(goes(xb)))
+            def _():
+                near_.start()
 
     finish(0)
 
     def third(i, _):
-        for k, (num, blk) in enumerate(((AIIP, xm), (AIIM, xp), (AIII, xo))):
-
-            @pl.when(i == k + 1)
-            def _():
-                got(a_at(blk, 2 * (1 - zlo)), num)
-
-        unit(order(i), 2 * (1 - zlo))
-        return 0
-
-    lax.fori_loop(1, 4, third, 0)
-    far_q = 2 * (1 - zlo) + 1
-    got(a_at(xm, far_q), AIIP + 1)
-    relay(a_at(xm, far_q, TPD - 2 * BYX, BYX), AFP, dev(x_=xp))
-    got(a_at(xp, far_q), AIIM + 1)
-    relay(a_at(xp, far_q, TPD - BYX, BYX), AFM, dev(x_=xm))
-
-    def last(i, _):
         @pl.when(i == 3)
         def _():
-            got(a_at(xo, far_q, 0, TPD - 2 * BYX), AIII + 1)
-            got(a_at(xo, far_q, TPD - 2 * BYX, BYX), AFP)
-            got(a_at(xo, far_q, TPD - BYX, BYX), AFM)
-
-        unit(order(i), far_q)
+            got(a_at(xo, far_q[0], 0, TPD - 2 * BYX), AIII)
+            got(a_at(xo, far_q[0], TPD - 2 * BYX, BYX), AFP)
+            got(a_at(xo, far_q[0], TPD - BYX, BYX), AFM)
+
+        unit(order(i), far_q[0])
+        return 0
+
+    lax.fori_loop(1, 4, third, 0)
+
+    def upper(i, _):
+        for k, (num, blk) in enumerate(((AIIP, xm), (AIIM, xp))):
+
+            @pl.when(i == k + 1)
+            def _():
+                got(a_at(blk, far_q[1], 0, MID), num + 1)
+
+        unit(order(i), far_q[1], 0, MID)
+        return 0
+
+    lax.fori_loop(1, 3, upper, 0)
+
+    got(a_at(xo, far_q[1], 0, MID), AIII + 1)
+    got(a_at(xo, far_q[1], MID, MID), AIV)
+    unit(xo, far_q[1])
+    finish(3)
+
+    def last(i, _):
+        for k, (num, blk) in enumerate(((ALP, xm), (ALM, xp))):
+
+            @pl.when(i == k + 1)
+            def _():
+                got(a_at(blk, far_q[1], MID, MID), num)
+
+        unit(order(i), far_q[1], MID, MID)
         finish(i)
         return 0
 
-    lax.fori_loop(1, 4, last, 0)
+    lax.fori_loop(1, 3, last, 0)
 
     for e in range(2):
         for r in range(2):
             got(out.at[pl.ds(r * TPD, TPD), pl.ds(e * NC, NC)], OUT + 2 * e + r)
-    for num in (AXP, AXP + 1, AXM, AXM + 1, AD, AOP, AOM, AIIP, AIIP + 1, AIIM, AIIM + 1, AIII):
+    for num in (AXP, AXP + 1, AXM, AXM + 1, AD, AIIP, AIIM):
         sent(a_at(x, t), num)
-    sent(a_at(x, t, 0, TPD - 2 * BYX), AIII + 1)
+    sent(a_at(x, t, 0, TPD - 2 * BYX), AIII)
+    for num in (AOP, AOM, AQP, AQM, AIII + 1, AIV, AIIP + 1, AIIM + 1, ALP, ALM):
+        sent(a_at(x, t, 0, MID), num)
     for r in range(2):
         sent(a_at(x, t), AZ + r)
     for num in (AFP, AFM):
@@ -380,11 +443,10 @@
     for num in range(DYM, OUT):
         sent(b_at(x, y, 0, 4), num)
     for i in range(4):
-        away, far, _ = out_copy(order(i), i)
-
-        @pl.when(away)
+
+        @pl.when(goes(order(i)))
         def _():
-            far.wait_send()
+            sent(obuf.at[i], OUT + i)
 
 
 def per_device(tokens, block_mask, norm_gain, w_query, w_key, w_value, query_gain, key_gain):
@@ -392,9 +454,9 @@
     hbm = pl.BlockSpec(memory_space=pl.ANY)
     return pl.pallas_call(
         kernel,
-        out_shape=jax.ShapeDtypeStruct((512, 768), jnp.bfloat16),
+        out_shape=pltpu.VMEM((512, 768), jnp.bfloat16),
         in_specs=[hbm, vmem, vmem, hbm, hbm, hbm, vmem, vmem],
-        out_specs=hbm,
+        out_specs=vmem,
         scratch_shapes=[
             pltpu.VMEM((2 * TPD, FEAT), jnp.bfloat16),
             pltpu.VMEM((2 * TPD, FEAT), jnp.bfloat16),

time: 123 us -> 123 us (level)
  the two profiles are of different devices: /device:TPU:32 before, /device:TPU:1 now
where the time goes in v4:
time: 123 us; the launch traced here: 121 us
  Pallas kernels  120 us (98%)
    pallas_call x1, Pallas kernels, per_device(): pl.pallas_call(kernel, out_shape=pltpu.VMEM((512, 768), jnp.bfloat16), in...  120 us

profile of v4, /device:TPU:1, one launch (start us, length us, event | category | flops | bytes accessed | tf_op | source)
XLA Modules:
  0.0 121.3 jit_solution(15032756638898107354)
XLA Ops:
  0.0 120.4 %shard_map.82 = bf16[512,768]{1,0:T(8,128)(2,1)S(1)} custom-call(bf16[512,1536]{1,0:T(8,128)(2,1)} %tok.1, s32[2,4,4]{2,1,0:T(4,128)} %bm.1, f32[1,6144]{1,0:T(1,128)} %bitcast.3, bf16[96,768]{1,0:T(8,128)(2,1)} %wq.1, bf16[96,768]{1,0:T(8,128)(2,1)} %wk.1, bf16[96,768]{1,0:T(8,128)(2,1)} %wv.1, f32[1,128]{1,0:T(1,128)} %bitcast.4, f32[1,128]{1,0:T(1,128)} %bitcast.5), custom_call_target="tpu_custom_call" | custom-call | tf_op jit(solution)/shard_map/pallas_call | solution.py:455
  120.4 0.9 copy.10

commit v5 on v4

--- a/solution.py
+++ b/solution.py
@@ -34,7 +34,8 @@
 ALP, ALM = 77, 78
 AQP, AQM, AIV = 79, 80, 81
 COUNT = 82
-BYX = 96
+BP, BM = 64, 128
+BZ = TPD - BP - BM
 
 
 def kernel(
@@ -293,7 +294,7 @@
         for h in range(2):
             relay(b_at(xw[h], yy, 0, 4), base + h, dev(c_=1 - c))
     got(a_at(xo, near_q[0], 0, MID), AOP)
-    relay(a_at(xo, near_q[0], 0, TPD - 2 * BYX), AIII, dev(zlo_=1 - zlo))
+    relay(a_at(xo, near_q[0], 0, BZ), AIII, dev(zlo_=1 - zlo))
     got(a_at(xo, near_q[1], 0, MID), AQP)
     relay(a_at(xo, near_q[1], 0, MID), AIII + 1, dev(zlo_=1 - zlo))
     got(a_at(xo, near_q[1], MID, MID), AQM)
@@ -311,9 +312,9 @@
             got(b_at(xw[h], yo, names[k]), num + k)
         relay(b_at(xw[h], yo, 0, 4), DYO + h, dev(c_=1 - c))
     got(a_at(xm, far_q[0]), AIIP)
-    relay(a_at(xm, far_q[0], TPD - 2 * BYX, BYX), AFP, dev(x_=xp))
+    relay(a_at(xm, far_q[0], BZ, BP), AFP, dev(x_=xp))
     got(a_at(xp, far_q[0]), AIIM)
-    relay(a_at(xp, far_q[0], TPD - BYX, BYX), AFM, dev(x_=xm))
+    relay(a_at(xp, far_q[0], BZ + BP, BM), AFM, dev(x_=xm))
     pair_on(1, ALP, ALM, MID, MID)
     lax.fori_loop(0, 3, across, 0)
     for h in range(2):
@@ -378,9 +379,9 @@
     def third(i, _):
         @pl.when(i == 3)
         def _():
-            got(a_at(xo, far_q[0], 0, TPD - 2 * BYX), AIII)
-            got(a_at(xo, far_q[0], TPD - 2 * BYX, BYX), AFP)
-            got(a_at(xo, far_q[0], TPD - BYX, BYX), AFM)
+            got(a_at(xo, far_q[0], 0, BZ), AIII)
+            got(a_at(xo, far_q[0], BZ, BP), AFP)
+            got(a_at(xo, far_q[0], BZ + BP, BM), AFM)
 
         unit(order(i), far_q[0])
         return 0
@@ -422,13 +423,13 @@
             got(out.at[pl.ds(r * TPD, TPD), pl.ds(e * NC, NC)], OUT + 2 * e + r)
     for num in (AXP, AXP + 1, AXM, AXM + 1, AD, AIIP, AIIM):
         sent(a_at(x, t), num)
-    sent(a_at(x, t, 0, TPD - 2 * BYX), AIII)
+    sent(a_at(x, t, 0, BZ), AIII)
     for num in (AOP, AOM, AQP, AQM, AIII + 1, AIV, AIIP + 1, AIIM + 1, ALP, ALM):
         sent(a_at(x, t, 0, MID), num)
     for r in range(2):
         sent(a_at(x, t), AZ + r)
-    for num in (AFP, AFM):
-        sent(a_at(x, t, 0, BYX), num)
+    sent(a_at(x, t, 0, BP), AFP)
+    sent(a_at(x, t, 0, BM), AFM)
     for k in range(3):
         sent(mk, MK + k)
         sent(sg.at[t], ST + k)

time: 123 us -> 122 us (level)
  no operation moved by 1% of the time
where the time goes in v5:
time: 122 us; the launch traced here: 121 us
  Pallas kernels  121 us (99%)
    pallas_call x1, Pallas kernels, per_device(): pl.pallas_call(kernel, out_shape=pltpu.VMEM((512, 768), jnp.bfloat16), in...  121 us

profile of v5, /device:TPU:1, one launch (start us, length us, event | category | flops | bytes accessed | tf_op | source)
XLA Modules:
  0.0 121.4 jit_solution(17279591858965681669)
XLA Ops:
  0.0 120.5 %shard_map.82 = bf16[512,768]{1,0:T(8,128)(2,1)S(1)} custom-call(bf16[512,1536]{1,0:T(8,128)(2,1)} %tok.1, s32[2,4,4]{2,1,0:T(4,128)} %bm.1, f32[1,6144]{1,0:T(1,128)} %bitcast.3, bf16[96,768]{1,0:T(8,128)(2,1)} %wq.1, bf16[96,768]{1,0:T(8,128)(2,1)} %wk.1, bf16[96,768]{1,0:T(8,128)(2,1)} %wv.1, f32[1,128]{1,0:T(1,128)} %bitcast.4, f32[1,128]{1,0:T(1,128)} %bitcast.5), custom_call_target="tpu_custom_call" | custom-call | tf_op jit(solution)/shard_map/pallas_call | solution.py:456
  120.6 0.9 copy.10

commit v6 on v5

--- a/solution.py
+++ b/solution.py
@@ -34,7 +34,7 @@
 ALP, ALM = 77, 78
 AQP, AQM, AIV = 79, 80, 81
 COUNT = 82
-BP, BM = 64, 128
+BP, BM = 64, 112
 BZ = TPD - BP - BM
 
 

time: 122 us -> 121 us (level)
  Pallas kernels: 121 us -> 119 us
where the time goes in v6:
time: 121 us; the launch traced here: 120 us
  Pallas kernels  119 us (98%)
    pallas_call x1, Pallas kernels, per_device(): pl.pallas_call(kernel, out_shape=pltpu.VMEM((512, 768), jnp.bfloat16), in...  119 us

profile of v6, /device:TPU:1, one launch (start us, length us, event | category | flops | bytes accessed | tf_op | source)
XLA Modules:
  0.0 120.4 jit_solution(7840127599799866440)
XLA Ops:
  0.0 119.5 %shard_map.82 = bf16[512,768]{1,0:T(8,128)(2,1)S(1)} custom-call(bf16[512,1536]{1,0:T(8,128)(2,1)} %tok.1, s32[2,4,4]{2,1,0:T(4,128)} %bm.1, f32[1,6144]{1,0:T(1,128)} %bitcast.3, bf16[96,768]{1,0:T(8,128)(2,1)} %wq.1, bf16[96,768]{1,0:T(8,128)(2,1)} %wk.1, bf16[96,768]{1,0:T(8,128)(2,1)} %wv.1, f32[1,128]{1,0:T(1,128)} %bitcast.4, f32[1,128]{1,0:T(1,128)} %bitcast.5), custom_call_target="tpu_custom_call" | custom-call | tf_op jit(solution)/shard_map/pallas_call | solution.py:456
  119.5 0.9 copy.10
